TPU v7x, 256 devices: a whole 4x4x8 slice. The times are simulated.
256 devices in a mesh: fsdp: 8 (over z_hi, y), tensor: 32 (over x, z_lo, core).
Axes of the slice: x: 4, y: 4, z: 8 (z_hi: 2, z_lo: 4; z = z_hi * 4 + z_lo), core: 2. Of those that a mesh axis runs over, the one named last changes fastest.
Arguments:
- momentum: bfloat16 [8192, 28672], P('fsdp', 'tensor'), may hold values from -6 to 6
- gradient: bfloat16 [8192, 28672], P('fsdp', 'tensor'), may hold values from -4 to 4
- factor: float32 [28672, 512], P('tensor', 'fsdp'), may hold values from -0.03125 to 0.03125
Outputs:
- new_momentum: bfloat16 [8192, 28672], P('fsdp', 'tensor')
- new_factor: float32 [28672, 512], P('tensor', 'fsdp')
- update: bfloat16 [8192, 28672], P('fsdp', 'tensor')
All inputs are finite; a program needn't handle non-finite values.
Results may differ from a plain program's by a relative error of at most 0.017.
Values may be sent and summed in bfloat16 or wider, within the bound.
No kernel may reach another device: no remote copies, remote signals or barrier semaphores. Data moves between devices by JAX's collectives and lax.ppermute only.
A program may use at most 64 MiB of HBM per device.

v0:
```python
import jax
import jax.numpy as jnp
from jax import lax
from jax.sharding import Mesh
from jax.sharding import PartitionSpec as P

D = 8192
FF = 28672
R = 512
TENSOR = ("tensor_0", "tensor_1", "tensor_2")
decay_rate = 0.95
epsilon = 1e-06


def from_everyone(value, axis):
    length = lax.axis_size(axis)
    return lax.all_to_all(
        jnp.broadcast_to(value[None], (length, *value.shape)), axis, 0, 0, tiled=True
    )


def laid_out(pieces, dim):
    lengths = list(pieces.shape[1:])
    lengths[dim] *= pieces.shape[0]
    return jnp.moveaxis(pieces, 0, dim).reshape(lengths)


def collect(value, axis, dim):
    pieces = from_everyone(value, axis)
    return laid_out(pieces, dim)


def padded_to(lines, length):
    spare = -lines.shape[0] % length
    if not spare:
        return lines
    return jnp.concatenate([lines, jnp.zeros((spare, *lines.shape[1:]), lines.dtype)])


def gather_axes(value, axes, dim):
    far, near = axes
    leading = from_everyone(value, far)
    pieces = jnp.swapaxes(from_everyone(leading, near), 0, 1)
    return laid_out(pieces.reshape(-1, *value.shape), dim)


def in_blocks(value, dim, length):
    before, after = (value.shape[:dim], value.shape[dim + 1 :])
    return jnp.moveaxis(value.reshape(*before, length, -1, *after), dim, 0)


def sum_at_owner(value, axis, dim):
    length = lax.axis_size(axis)
    pieces = lax.all_to_all(in_blocks(value, dim, length), axis, 0, 0, tiled=True)
    return jnp.sum(pieces, axis=0)


def sum_by_axis(value, axes, dim):
    far, near = axes
    pieces = in_blocks(value, dim, lax.axis_size(far))
    nearer = sum_at_owner(pieces, near, dim + 1)
    arrived = lax.all_to_all(nearer, far, split_axis=0, concat_axis=0, tiled=True)
    return arrived.sum(axis=0)


def sum_by_parts(value, axes):
    lines = value.reshape(-1, value.shape[-1])
    padded = padded_to(lines, lax.axis_size(axes[0]) * lax.axis_size(axes[1]))
    whole = gather_axes(sum_by_axis(padded, axes, 0), axes, 0)
    return lax.slice_in_dim(whole, 0, len(lines)).reshape(value.shape)


def over_copies(value, axis):
    everything = from_everyone(value, axis)
    return jnp.sum(everything, axis=0)


def on_device(momentum, gradient, factor):
    blended = (momentum.astype(jnp.float32) + gradient.astype(jnp.float32)).astype(jnp.bfloat16)
    lowered = factor.astype(jnp.bfloat16)
    columns = factor.shape[1]
    partial_left = jnp.dot(blended, collect(lowered, "fsdp", 1), preferred_element_type=jnp.float32)
    left_factor = sum_by_parts(partial_left, (("tensor_0", "tensor_1"), "tensor_2"))
    local_gram = lax.dot_general(
        left_factor, left_factor, (((0,), (0,)), ((), ())), precision=lax.Precision.HIGHEST
    )
    gram_matrix = lax.psum(local_gram, "fsdp")
    lower_factor = jnp.linalg.cholesky(gram_matrix)
    solved = jax.scipy.linalg.solve_triangular(lower_factor, left_factor.T, lower=True)
    orthonormal = solved.T.astype(jnp.bfloat16)
    partial_right = lax.dot_general(
        blended, orthonormal, (((0,), (0,)), ((), ())), preferred_element_type=jnp.float32
    )
    right_factor = lax.psum(partial_right.astype(jnp.bfloat16), "fsdp").astype(jnp.float32)
    square_sums = over_copies(jnp.sum(right_factor * right_factor, axis=0), TENSOR)
    inverse = lax.rsqrt(square_sums + epsilon)
    full_factor = right_factor * inverse[None, :]
    own_factor = lax.dynamic_slice_in_dim(full_factor, lax.axis_index("fsdp") * columns, columns, 1)
    product = lax.dot_general(
        orthonormal,
        right_factor.astype(jnp.bfloat16),
        (((1,), (1,)), ((), ())),
        preferred_element_type=jnp.float32,
    )
    stepped = lax.dot_general(
        orthonormal,
        full_factor.astype(jnp.bfloat16),
        (((1,), (1,)), ((), ())),
        preferred_element_type=jnp.float32,
    )
    new_momentum = (blended.astype(jnp.float32) - (1.0 - decay_rate) * product).astype(jnp.bfloat16)
    update = (stepped * jnp.sqrt(jnp.float32(D * FF / R))).astype(jnp.bfloat16)
    return (new_momentum, own_factor, update)


def solution(mesh):
    torus = Mesh(
        mesh.devices.reshape(mesh.shape["fsdp"], 4, 4, 2),
        ("fsdp", "tensor_0", "tensor_1", "tensor_2"),
    )
    return jax.shard_map(
        on_device,
        mesh=torus,
        in_specs=(P("fsdp", TENSOR), P("fsdp", TENSOR), P(TENSOR, "fsdp")),
        out_specs=(P("fsdp", TENSOR), P(TENSOR, "fsdp"), P("fsdp", TENSOR)),
        check_vma=False,
    )
```

profile of v0, /device:TPU:1, one launch (start us, length us, event | category | flops | bytes accessed | tf_op | source)
XLA Modules:
  0.0 529.0 jit_solution(15417045091283632723)
XLA Ops:
  9.3 11.6 %all-to-all-start = ((bf16[8,896,64]{1,2,0:T(8,128)(2,1)}), bf16[8,896,64]{1,2,0:T(8,128)(2,1)S(1)}, u32[]{:S(2)}, u32[]{:S(2)}) async-start(bf16[8,896,64]{1,2,0:T(8,128)(2,1)} %broadcast_in_dim.9), calls=%async_computation | async-start | bytes 1835008 | tf_op jit(solution)/shard_map/all_to_all | solution.py:17
  21.0 3.2 add_convert_fusion
  24.2 13.0 %all-to-all-done = bf16[8,896,64]{1,2,0:T(8,128)(2,1)S(1)} async-done(((bf16[8,896,64]{1,2,0:T(8,128)(2,1)}), bf16[8,896,64]{1,2,0:T(8,128)(2,1)S(1)}, u32[]{:S(2)}, u32[]{:S(2)}) %all-to-all-start) | async-done | bytes 917536 | tf_op jit(solution)/shard_map/all_to_all | solution.py:17
  37.2 2.8 convolution_bitcast_fusion
  40.3 11.2 %all_to_all.31 = f32[2,16,32,512]{3,2,1,0:T(8,128)S(1)} all-to-all(f32[2,16,32,512]{3,2,1,0:T(8,128)S(1)} %copy.29), channel_id=1, replica_groups=mesh['fsdp'=8,'tensor_0'=4,'tensor_1'=4,'tensor_2'=2] {'tensor_2'}, dimensions={0} | all-to-all | bytes 4194304 | tf_op jit(solution)/shard_map/all_to_all | solution.py:54
  51.8 37.0 %all_to_all.32 = f32[16,32,512]{2,1,0:T(8,128)S(1)} all-to-all(f32[16,32,512]{2,1,0:T(8,128)S(1)} %reduce_sum.36), channel_id=1, replica_groups=mesh['fsdp'=8,'tensor_0'=4,'tensor_1'=4,'tensor_2'=2] {'tensor_0','tenso..., dimensions={0} | all-to-all | bytes 2097152 | tf_op jit(solution)/shard_map/all_to_all | solution.py:62
  88.9 30.9 %all_to_all.33 = f32[16,32,512]{2,1,0:T(8,128)S(1)} all-to-all(f32[16,32,512]{2,1,0:T(8,128)S(1)} %broadcast_in_dim.10), channel_id=1, replica_groups=mesh['fsdp'=8,'tensor_0'=4,'tensor_1'=4,'tensor_2'=2] {'tensor_0','tenso..., dimensions={0} | all-to-all | bytes 2097152 | tf_op jit(solution)/shard_map/all_to_all | solution.py:17
  120.1 6.8 %all_to_all.34 = f32[2,16,32,512]{3,2,1,0:T(8,128)S(1)} all-to-all(f32[2,16,32,512]{3,2,1,0:T(8,128)S(1)} %broadcast_in_dim.11), channel_id=1, replica_groups=mesh['fsdp'=8,'tensor_0'=4,'tensor_1'=4,'tensor_2'=2] {'tensor_2'}, dimensions={0} | all-to-all | bytes 4194304 | tf_op jit(solution)/shard_map/all_to_all | solution.py:17
  126.8 4.5 fusion.9
  133.0 2.4 copy.33
  135.4 97.5 %all-reduce.4.cloned.1.call-done = f32[512,512]{0,1:T(8,128)} async-done(((f32[512,512]{0,1:T(8,128)}), f32[512,512]{0,1:T(8,128)}) %all-reduce.4.cloned.1.call-update) | async-done | bytes 1048592 | tf_op jit(solution)/shard_map/psum | solution.py:87
  232.9 2.6 copy.32
  238.0 11.7 %cholesky.104 = f32[128,128]{1,0:T(8,128)S(1)} custom-call(f32[128,128]{1,0:T(8,128)S(1)} %cholesky.266), custom_call_target="Cholesky" | custom-call | tf_op jit(solution)/shard_map/jit(cholesky)/cholesky | solution.py:88
  249.8 9.8 %custom-call.31 = f32[1,128,128]{1,2,0:T(8,128)S(1)} custom-call(f32[1,128,128]{2,1,0:T(8,128)S(1)} %get-tuple-element.45), custom_call_target="InvertDiagBlocksLowerTriangular" | custom-call | tf_op jit(solution)/shard_map/jit(cholesky)/cholesky | solution.py:88
  262.2 11.7 %cholesky.217 = f32[128,128]{1,0:T(8,128)S(1)} custom-call(f32[128,128]{1,0:T(8,128)S(1)} %cholesky.270), custom_call_target="Cholesky" | custom-call | tf_op jit(solution)/shard_map/jit(cholesky)/cholesky | solution.py:88
  273.9 10.0 %custom-call.32 = f32[1,128,128]{1,2,0:T(8,128)S(1)} custom-call(f32[1,128,128]{2,1,0:T(8,128)S(1)} %get-tuple-element.42), custom_call_target="InvertDiagBlocksLowerTriangular" | custom-call | tf_op jit(solution)/shard_map/jit(cholesky)/cholesky | solution.py:88
  285.4 11.7 %cholesky.238 = f32[128,128]{1,0:T(8,128)S(1)} custom-call(f32[128,128]{1,0:T(8,128)S(1)} %cholesky.275), custom_call_target="Cholesky" | custom-call | tf_op jit(solution)/shard_map/jit(cholesky)/cholesky | solution.py:88
  297.9 9.8 %custom-call.33 = f32[1,128,128]{1,2,0:T(8,128)S(1)} custom-call(f32[1,128,128]{2,1,0:T(8,128)S(1)} %get-tuple-element.39), custom_call_target="InvertDiagBlocksLowerTriangular" | custom-call | tf_op jit(solution)/shard_map/jit(cholesky)/cholesky | solution.py:88
  309.2 11.7 %cholesky.255 = f32[128,128]{1,0:T(8,128)S(1)} custom-call(f32[128,128]{1,0:T(8,128)S(1)} %convolution_subtract_fusion.4), custom_call_target="Cholesky" | custom-call | tf_op jit(solution)/shard_map/jit(cholesky)/cholesky | solution.py:88
  326.1 14.1 %while.1 = (s32[]{:T(128)}, f32[512,512]{1,0:T(8,128)}, s32[4,2]{0,1:T(2,128)S(1)}, f32[4,128,128]{2,1,0:T(8,128)}, s32[]{:T(128)}) while((s32[]{:T(128)}, f32[512,512]{1,0:T(8,128)}, s32[4,2]{0,1:T(2,128)S(1)}, f32[4,128,128]{2,1,0:T(8,128)}, s32[]{:T(128)}) %tuple.39), condition=%wide.while_cond, body=%wide.while_body.sunk | while | flops 2 | bytes 132705 | solution.py:89
  326.7 2.9 bitcast_dynamic-update-slice_fusion.2
  330.3 2.9 bitcast_dynamic-update-slice_fusion.2
  333.8 2.9 bitcast_dynamic-update-slice_fusion.2
  337.4 2.8 bitcast_dynamic-update-slice_fusion.2
  340.2 40.1 %custom-call.34 = f32[4,128,128]{1,2,0:T(8,128)S(1)} custom-call(f32[4,128,128]{2,1,0:T(8,128)} %get-tuple-element.10), custom_call_target="InvertDiagBlocksLowerTriangular" | custom-call | tf_op jit(solution)/shard_map/jit(_solve_triangular)/triangular_solve | solution.py:89
  385.4 2.2 fusion.12
  388.2 2.1 convolution_convert_fusion
  390.4 106.7 %all-reduce.6.cloned.1.call-done = bf16[896,512]{1,0:T(8,128)(2,1)} async-done(((bf16[896,512]{1,0:T(8,128)(2,1)}), bf16[896,512]{1,0:T(8,128)(2,1)}) %all-reduce.6.cloned.1.call-update) | async-done | bytes 917520 | tf_op jit(solution)/shard_map/psum | solution.py:94
  499.2 11.0 %all-to-all-start.5 = ((f32[32,1,512]{2,1,0:T(1,128)}), f32[32,1,512]{2,1,0:T(1,128)S(1)}, u32[]{:S(2)}, u32[]{:S(2)}) async-start(f32[32,1,512]{2,1,0:T(1,128)} %broadcast_in_dim.12), calls=%async_computation.5 | async-start | bytes 131072 | tf_op jit(solution)/shard_map/all_to_all | solution.py:17
  510.2 4.0 subtract_convert_fusion
  514.2 3.8 all-to-all-done.5
  519.4 2.5 multiply_convert_fusion
  (75 shorter events, 28.2 us)
Async XLA Ops:
  7.2 13.8 %copy-start.3 = (bf16[1024,896]{1,0:T(8,128)(2,1)S(1)}, bf16[1024,896]{1,0:T(8,128)(2,1)}, u32[]{:S(2)}) copy-start(bf16[1024,896]{1,0:T(8,128)(2,1)} %param.4) | copy-start | bytes 5505028
  9.3 27.9 %all-to-all-start = ((bf16[8,896,64]{1,2,0:T(8,128)(2,1)}), bf16[8,896,64]{1,2,0:T(8,128)(2,1)S(1)}, u32[]{:S(2)}, u32[]{:S(2)}) async-start(bf16[8,896,64]{1,2,0:T(8,128)(2,1)} %broadcast_in_dim.9), calls=%async_computation | async-start | bytes 1835008 | tf_op jit(solution)/shard_map/all_to_all | solution.py:17
  21.0 211.9 %all-reduce.4.cloned.1.call-start = ((), (), s32[]{:S(2)}) async-start(), calls=%async_computation.6 | async-start | bytes 2097152 | tf_op jit(solution)/shard_map/psum | solution.py:87
  131.4 365.7 %all-reduce.6.cloned.1.call-start = ((), (), s32[]{:S(2)}) async-start(), calls=%async_computation.7 | async-start | bytes 1835008 | tf_op jit(solution)/shard_map/psum | solution.py:94
  232.9 2.6 copy-start
  237.0 1.0 copy-start.2
  383.0 5.2 copy-start.6
  385.4 2.8 copy-start.8
  385.4 2.8 copy-start.4
  388.2 122.0 %copy-start.5 = (bf16[1024,896]{1,0:T(8,128)(2,1)S(1)}, bf16[1024,896]{1,0:T(8,128)(2,1)}, u32[]{:S(2)}) copy-start(bf16[1024,896]{1,0:T(8,128)(2,1)} %add_convert_fusion) | copy-start | bytes 5505028
  499.2 18.8 %all-to-all-start.5 = ((f32[32,1,512]{2,1,0:T(1,128)}), f32[32,1,512]{2,1,0:T(1,128)S(1)}, u32[]{:S(2)}, u32[]{:S(2)}) async-start(f32[32,1,512]{2,1,0:T(1,128)} %broadcast_in_dim.12), calls=%async_computation.5 | async-start | bytes 131072 | tf_op jit(solution)/shard_map/all_to_all | solution.py:17
  510.2 7.9 %copy-start.1 = (bf16[896,512]{1,0:T(8,128)(2,1)S(1)}, bf16[896,512]{1,0:T(8,128)(2,1)}, u32[]{:S(2)}) copy-start(bf16[896,512]{1,0:T(8,128)(2,1)} %all-reduce.6.cloned.1.call-done) | copy-start | bytes 2752516
  518.1 1.3 copy-start.7
  518.1 1.3 copy-start.9
Sparse Core Ops, SparseCore 0:
  131.5 101.3 all-reduce.3
  390.5 106.5 all-reduce.5
where the time goes:
time: 536 us; the launch traced here: 529 us
  waiting for transfers between devices  221 us (41%)
  other arithmetic  128 us (24%)
  blocking collectives  85.8 us (16%)
  matrix products  29.2 us (5%)
  local copies, waits for them, and re-layouts  25.2 us (5%)
  starting transfers between devices  22.7 us (4%)
  between operations  17.2 us (3%)
    psum x1, waiting for transfers between devices, on_device(): lax.psum(partial_right.astype(jnp.bfloat16), 'fsdp').astype(jnp.float32)  107 us
    psum x1, waiting for transfers between devices, on_device(): gram_matrix = lax.psum(local_gram, 'fsdp')  97.5 us
    another operation x14, other arithmetic, on_device(): lower_factor = jnp.linalg.cholesky(gram_matrix)  78.6 us
    another operation x3, other arithmetic, on_device(): jax.scipy.linalg.solve_triangular(lower_factor, left_factor.T, lower=True)  41.4 us
    all_to_all x2, blocking collectives, from_everyone(): lax.all_to_all(jnp.broadcast_to(value[None], (length, *value.shape)), axi...  37.6 us
    all_to_all x1, blocking collectives, sum_by_axis(): lax.all_to_all(nearer, far, split_axis=0, concat_axis=0, tiled=True)  37 us
    all_to_all x2, starting transfers between devices, from_everyone(): lax.all_to_all(jnp.broadcast_to(value[None], (length, *value.shape)), axi...  22.7 us
    all_to_all x2, waiting for transfers between devices, from_everyone(): lax.all_to_all(jnp.broadcast_to(value[None], (length, *value.shape)), axi...  16.8 us
  transfers between devices with their start and end apart: 4, of which 4 were waited for; matrix products, arithmetic and copies ran while one was open for 2% of the time, Pallas kernels for 0%

commit v1 on v0

--- a/solution.py
+++ b/solution.py
@@ -84,7 +84,7 @@
     local_gram = lax.dot_general(
         left_factor, left_factor, (((0,), (0,)), ((), ())), precision=lax.Precision.HIGHEST
     )
-    gram_matrix = lax.psum(local_gram, "fsdp")
+    gram_matrix = jnp.sum(lax.all_gather(local_gram, "fsdp"), axis=0)
     lower_factor = jnp.linalg.cholesky(gram_matrix)
     solved = jax.scipy.linalg.solve_triangular(lower_factor, left_factor.T, lower=True)
     orthonormal = solved.T.astype(jnp.bfloat16)

time: 536 us -> 599 us (1.12)
  waiting for transfers between devices: 221 us -> 281 us
    all_gather x0 -> x1, waiting for transfers between devices: none -> 163 us  [on_device(): gram_matrix = jnp.sum(lax.all_gather(local_gram, 'fsdp'), axis=0)]
    psum x1 -> x0, waiting for transfers between devices: 97.5 us -> none  [on_device(): gram_matrix = lax.psum(local_gram, 'fsdp')]
where the time goes in v1:
time: 599 us; the launch traced here: 592 us
  waiting for transfers between devices  281 us (47%)
  other arithmetic  132 us (22%)
  blocking collectives  85.8 us (14%)
  matrix products  29.2 us (5%)
  local copies, waits for them, and re-layouts  24 us (4%)
  starting transfers between devices  23.1 us (4%)
  between operations  17.2 us (3%)
    all_gather x1, waiting for transfers between devices, on_device(): gram_matrix = jnp.sum(lax.all_gather(local_gram, 'fsdp'), axis=0)  163 us
    psum x1, waiting for transfers between devices, on_device(): lax.psum(partial_right.astype(jnp.bfloat16), 'fsdp').astype(jnp.float32)  101 us
    another operation x14, other arithmetic, on_device(): lower_factor = jnp.linalg.cholesky(gram_matrix)  78.8 us
    another operation x3, other arithmetic, on_device(): jax.scipy.linalg.solve_triangular(lower_factor, left_factor.T, lower=True)  41.2 us
    all_to_all x2, blocking collectives, from_everyone(): lax.all_to_all(jnp.broadcast_to(value[None], (length, *value.shape)), axi...  37.6 us
    all_to_all x1, blocking collectives, sum_by_axis(): lax.all_to_all(nearer, far, split_axis=0, concat_axis=0, tiled=True)  37 us
    all_to_all x2, starting transfers between devices, from_everyone(): lax.all_to_all(jnp.broadcast_to(value[None], (length, *value.shape)), axi...  23 us
    all_to_all x2, waiting for transfers between devices, from_everyone(): lax.all_to_all(jnp.broadcast_to(value[None], (length, *value.shape)), axi...  16.7 us
  transfers between devices with their start and end apart: 4, of which 4 were waited for; matrix products, arithmetic and copies ran while one was open for 2% of the time, Pallas kernels for 0%

profile of v1, /device:TPU:1, one launch (start us, length us, event | category | flops | bytes accessed | tf_op | source)
XLA Modules:
  0.0 592.4 jit_solution(1439421644321437870)
XLA Ops:
  9.3 11.6 %all-to-all-start = ((bf16[8,896,64]{1,2,0:T(8,128)(2,1)}), bf16[8,896,64]{1,2,0:T(8,128)(2,1)S(1)}, u32[]{:S(2)}, u32[]{:S(2)}) async-start(bf16[8,896,64]{1,2,0:T(8,128)(2,1)} %broadcast_in_dim.9), calls=%async_computation | async-start | bytes 1835008 | tf_op jit(solution)/shard_map/all_to_all | solution.py:17
  21.0 3.2 add_convert_fusion
  24.2 13.0 %all-to-all-done = bf16[8,896,64]{1,2,0:T(8,128)(2,1)S(1)} async-done(((bf16[8,896,64]{1,2,0:T(8,128)(2,1)}), bf16[8,896,64]{1,2,0:T(8,128)(2,1)S(1)}, u32[]{:S(2)}, u32[]{:S(2)}) %all-to-all-start) | async-done | bytes 917536 | tf_op jit(solution)/shard_map/all_to_all | solution.py:17
  37.2 2.8 convolution_bitcast_fusion
  40.3 11.2 %all_to_all.31 = f32[2,16,32,512]{3,2,1,0:T(8,128)S(1)} all-to-all(f32[2,16,32,512]{3,2,1,0:T(8,128)S(1)} %copy.25), channel_id=1, replica_groups=mesh['fsdp'=8,'tensor_0'=4,'tensor_1'=4,'tensor_2'=2] {'tensor_2'}, dimensions={0} | all-to-all | bytes 4194304 | tf_op jit(solution)/shard_map/all_to_all | solution.py:54
  51.8 37.0 %all_to_all.32 = f32[16,32,512]{2,1,0:T(8,128)S(1)} all-to-all(f32[16,32,512]{2,1,0:T(8,128)S(1)} %reduce_sum.45), channel_id=1, replica_groups=mesh['fsdp'=8,'tensor_0'=4,'tensor_1'=4,'tensor_2'=2] {'tensor_0','tenso..., dimensions={0} | all-to-all | bytes 2097152 | tf_op jit(solution)/shard_map/all_to_all | solution.py:62
  88.9 30.9 %all_to_all.33 = f32[16,32,512]{2,1,0:T(8,128)S(1)} all-to-all(f32[16,32,512]{2,1,0:T(8,128)S(1)} %broadcast_in_dim.10), channel_id=1, replica_groups=mesh['fsdp'=8,'tensor_0'=4,'tensor_1'=4,'tensor_2'=2] {'tensor_0','tenso..., dimensions={0} | all-to-all | bytes 2097152 | tf_op jit(solution)/shard_map/all_to_all | solution.py:17
  120.1 6.8 %all_to_all.34 = f32[2,16,32,512]{3,2,1,0:T(8,128)S(1)} all-to-all(f32[2,16,32,512]{3,2,1,0:T(8,128)S(1)} %broadcast_in_dim.11), channel_id=1, replica_groups=mesh['fsdp'=8,'tensor_0'=4,'tensor_1'=4,'tensor_2'=2] {'tensor_2'}, dimensions={0} | all-to-all | bytes 4194304 | tf_op jit(solution)/shard_map/all_to_all | solution.py:17
  126.8 4.5 fusion.9
  133.0 2.4 copy.28
  135.5 162.9 %all-gather.3.cloned.1.call-done = f32[4096,512]{1,0:T(8,128)} async-done(((f32[512,512]{1,0:T(8,128)}), f32[4096,512]{1,0:T(8,128)}) %all-gather.3.cloned.1.call-update) | async-done | bytes 8388624 | tf_op jit(solution)/shard_map/all_gather | solution.py:87
  298.3 4.5 reduce_sum.47
  306.6 11.7 %cholesky.104 = f32[128,128]{1,0:T(8,128)S(1)} custom-call(f32[128,128]{1,0:T(8,128)S(1)} %cholesky.266), custom_call_target="Cholesky" | custom-call | tf_op jit(solution)/shard_map/jit(cholesky)/cholesky | solution.py:88
  318.5 9.8 %custom-call.31 = f32[1,128,128]{1,2,0:T(8,128)S(1)} custom-call(f32[1,128,128]{2,1,0:T(8,128)S(1)} %get-tuple-element.45), custom_call_target="InvertDiagBlocksLowerTriangular" | custom-call | tf_op jit(solution)/shard_map/jit(cholesky)/cholesky | solution.py:88
  330.8 11.9 %cholesky.217 = f32[128,128]{1,0:T(8,128)S(1)} custom-call(f32[128,128]{1,0:T(8,128)S(1)} %cholesky.270), custom_call_target="Cholesky" | custom-call | tf_op jit(solution)/shard_map/jit(cholesky)/cholesky | solution.py:88
  342.7 9.8 %custom-call.32 = f32[1,128,128]{1,2,0:T(8,128)S(1)} custom-call(f32[1,128,128]{2,1,0:T(8,128)S(1)} %get-tuple-element.42), custom_call_target="InvertDiagBlocksLowerTriangular" | custom-call | tf_op jit(solution)/shard_map/jit(cholesky)/cholesky | solution.py:88
  354.1 11.7 %cholesky.238 = f32[128,128]{1,0:T(8,128)S(1)} custom-call(f32[128,128]{1,0:T(8,128)S(1)} %cholesky.275), custom_call_target="Cholesky" | custom-call | tf_op jit(solution)/shard_map/jit(cholesky)/cholesky | solution.py:88
  366.6 9.8 %custom-call.33 = f32[1,128,128]{1,2,0:T(8,128)S(1)} custom-call(f32[1,128,128]{2,1,0:T(8,128)S(1)} %get-tuple-element.39), custom_call_target="InvertDiagBlocksLowerTriangular" | custom-call | tf_op jit(solution)/shard_map/jit(cholesky)/cholesky | solution.py:88
  377.8 11.9 %cholesky.255 = f32[128,128]{1,0:T(8,128)S(1)} custom-call(f32[128,128]{1,0:T(8,128)S(1)} %convolution_subtract_fusion.4), custom_call_target="Cholesky" | custom-call | tf_op jit(solution)/shard_map/jit(cholesky)/cholesky | solution.py:88
  394.7 14.1 %while.1 = (s32[]{:T(128)}, f32[512,512]{1,0:T(8,128)}, s32[4,2]{0,1:T(2,128)S(1)}, f32[4,128,128]{2,1,0:T(8,128)}, s32[]{:T(128)}) while((s32[]{:T(128)}, f32[512,512]{1,0:T(8,128)}, s32[4,2]{0,1:T(2,128)S(1)}, f32[4,128,128]{2,1,0:T(8,128)}, s32[]{:T(128)}) %tuple.39), condition=%wide.while_cond, body=%wide.while_body.sunk | while | flops 2 | bytes 132705 | solution.py:89
  395.4 2.9 bitcast_dynamic-update-slice_fusion.2
  398.9 2.9 bitcast_dynamic-update-slice_fusion.2
  402.5 2.9 bitcast_dynamic-update-slice_fusion.2
  406.0 2.8 bitcast_dynamic-update-slice_fusion.2
  408.8 40.1 %custom-call.34 = f32[4,128,128]{1,2,0:T(8,128)S(1)} custom-call(f32[4,128,128]{2,1,0:T(8,128)} %get-tuple-element.10), custom_call_target="InvertDiagBlocksLowerTriangular" | custom-call | tf_op jit(solution)/shard_map/jit(_solve_triangular)/triangular_solve | solution.py:89
  454.0 2.2 fusion.12
  456.9 2.1 convolution_convert_fusion
  459.0 101.2 %all-reduce.3.cloned.1.call-done = bf16[896,512]{1,0:T(8,128)(2,1)} async-done(((bf16[896,512]{1,0:T(8,128)(2,1)}), bf16[896,512]{1,0:T(8,128)(2,1)}) %all-reduce.3.cloned.1.call-update) | async-done | bytes 917520 | tf_op jit(solution)/shard_map/psum | solution.py:94
  562.3 11.4 %all-to-all-start.5 = ((f32[32,1,512]{2,1,0:T(1,128)}), f32[32,1,512]{2,1,0:T(1,128)S(1)}, u32[]{:S(2)}, u32[]{:S(2)}) async-start(f32[32,1,512]{2,1,0:T(1,128)} %broadcast_in_dim.12), calls=%async_computation.5 | async-start | bytes 131072 | tf_op jit(solution)/shard_map/all_to_all | solution.py:17
  573.7 4.0 subtract_convert_fusion
  577.7 3.7 all-to-all-done.5
  582.8 2.5 multiply_convert_fusion
  (74 shorter events, 29.3 us)
Async XLA Ops:
  7.2 13.8 %copy-start.2 = (bf16[1024,896]{1,0:T(8,128)(2,1)S(1)}, bf16[1024,896]{1,0:T(8,128)(2,1)}, u32[]{:S(2)}) copy-start(bf16[1024,896]{1,0:T(8,128)(2,1)} %param.4) | copy-start | bytes 5505028
  9.3 27.9 %all-to-all-start = ((bf16[8,896,64]{1,2,0:T(8,128)(2,1)}), bf16[8,896,64]{1,2,0:T(8,128)(2,1)S(1)}, u32[]{:S(2)}, u32[]{:S(2)}) async-start(bf16[8,896,64]{1,2,0:T(8,128)(2,1)} %broadcast_in_dim.9), calls=%async_computation | async-start | bytes 1835008 | tf_op jit(solution)/shard_map/all_to_all | solution.py:17
  21.0 277.4 %all-gather.3.cloned.1.call-start = ((), (), s32[]{:S(2)}) async-start(), calls=%async_computation.7 | async-start | bytes 9437184 | tf_op jit(solution)/shard_map/all_gather | solution.py:87
  131.4 428.9 %all-reduce.3.cloned.1.call-start = ((), (), s32[]{:S(2)}) async-start(), calls=%async_computation.6 | async-start | bytes 1835008 | tf_op jit(solution)/shard_map/psum | solution.py:94
  305.6 1.0 copy-start.1
  451.6 5.2 copy-start.5
  454.0 2.8 copy-start.7
  454.0 2.8 copy-start.3
  456.9 116.8 %copy-start.4 = (bf16[1024,896]{1,0:T(8,128)(2,1)S(1)}, bf16[1024,896]{1,0:T(8,128)(2,1)}, u32[]{:S(2)}) copy-start(bf16[1024,896]{1,0:T(8,128)(2,1)} %add_convert_fusion) | copy-start | bytes 5505028
  562.3 19.0 %all-to-all-start.5 = ((f32[32,1,512]{2,1,0:T(1,128)}), f32[32,1,512]{2,1,0:T(1,128)S(1)}, u32[]{:S(2)}, u32[]{:S(2)}) async-start(f32[32,1,512]{2,1,0:T(1,128)} %broadcast_in_dim.12), calls=%async_computation.5 | async-start | bytes 131072 | tf_op jit(solution)/shard_map/all_to_all | solution.py:17
  573.7 7.7 %copy-start = (bf16[896,512]{1,0:T(8,128)(2,1)S(1)}, bf16[896,512]{1,0:T(8,128)(2,1)}, u32[]{:S(2)}) copy-start(bf16[896,512]{1,0:T(8,128)(2,1)} %all-reduce.3.cloned.1.call-done) | copy-start | bytes 2752516
  581.5 1.3 copy-start.6
  581.5 1.3 copy-start.8
Sparse Core Ops, SparseCore 0:
  131.5 166.8 all-gather.2
  459.1 101.0 all-reduce.2
